TPU v7x, 32 devices: a whole 2x2x4 slice. The times are simulated.
32 devices in a mesh: member: 2 (over x), fsdp: 16 (over z, y, core).
Axes of the slice: x: 2, y: 2, z: 4, core: 2. Of those that a mesh axis runs over, the one named last changes fastest.
Arguments:
- context: bfloat16 [4, 2048, 2048], P(None, 'fsdp', 'member'), may hold values from -6 to 6
- residual: bfloat16 [2048, 2048], P('fsdp', 'member'), may hold values from -6 to 6
- out_weight: bfloat16 [2048, 2048], P('fsdp', 'member'), may hold values from -0.1875 to 0.1875
- in_factor: bfloat16 [4, 2048], P(None, 'member'), may hold values from 0.25 to 1.75
- out_factor: bfloat16 [4, 2048], P(None, 'member'), may hold values from 0.25 to 1.75
- cotangent: bfloat16 [4, 2048, 2048], P(None, 'fsdp', 'member'), may hold values from -0.796875 to 0.796875
Outputs:
- hidden: bfloat16 [4, 2048, 2048], P(None, 'fsdp', 'member')
- grad_context: bfloat16 [4, 2048, 2048], P(None, 'fsdp', 'member')
- grad_weight: float32 [2048, 2048], P('fsdp', 'member')
- grad_in_factor: float32 [4, 2048], P(None, 'member')
- grad_out_factor: float32 [4, 2048], P(None, 'member')
- grad_residual: float32 [2048, 2048], P('fsdp', 'member')
All inputs are finite; a program needn't handle non-finite values.
Results may differ from a plain program's by a relative error of at most 0.013.
Values may be sent and summed in bfloat16 or wider, within the bound.
A program may use at most 64 MiB of HBM per device.

v0:
```python
import jax
import jax.numpy as jnp
from jax import lax
from jax.sharding import PartitionSpec as P


def per_device(context, residual, out_weight, in_factor, out_factor, cotangent):
    in_wide = in_factor.astype(jnp.float32)
    out_wide = out_factor.astype(jnp.float32)
    scaled_local = (context.astype(jnp.float32) * in_wide[:, None, :]).astype(jnp.bfloat16)
    scaled_grad = (cotangent.astype(jnp.float32) * out_wide[:, None, :]).astype(jnp.bfloat16)
    scaled_context = lax.all_gather(scaled_local, "member", axis=2, tiled=True)
    weight = lax.all_gather(out_weight, "fsdp", axis=0, tiled=True)
    projected = jnp.einsum(
        "eti,id->etd", scaled_context, weight, preferred_element_type=jnp.float32
    )
    partial_value = jnp.einsum(
        "etd,id->eti", scaled_grad, weight, preferred_element_type=jnp.float32
    )
    hidden = (residual.astype(jnp.float32)[None] + projected * out_wide[:, None, :]).astype(
        jnp.bfloat16
    )
    backward = lax.psum_scatter(
        partial_value.astype(jnp.bfloat16), "member", scatter_dimension=2, tiled=True
    ).astype(jnp.float32)
    grad_context = (backward * in_wide[:, None, :]).astype(jnp.bfloat16)
    grad_in_local = jnp.sum(context.astype(jnp.float32) * backward, axis=1)
    grad_out_local = jnp.sum(cotangent.astype(jnp.float32) * projected, axis=1)
    grad_in, grad_out = lax.psum((grad_in_local, grad_out_local), "fsdp")
    grad_block = jnp.einsum(
        "eti,etd->id", scaled_context, scaled_grad, preferred_element_type=jnp.float32
    )
    grad_weight = lax.psum_scatter(grad_block, "fsdp", scatter_dimension=0, tiled=True)
    grad_residual = jnp.sum(cotangent.astype(jnp.float32), axis=0)
    return (hidden, grad_context, grad_weight, grad_in, grad_out, grad_residual)


def solution(mesh):
    in_specs = (
        P(None, "fsdp", "member"),
        P("fsdp", "member"),
        P("fsdp", "member"),
        P(None, "member"),
        P(None, "member"),
        P(None, "fsdp", "member"),
    )
    out_specs = (
        P(None, "fsdp", "member"),
        P(None, "fsdp", "member"),
        P("fsdp", "member"),
        P(None, "member"),
        P(None, "member"),
        P("fsdp", "member"),
    )
    return jax.shard_map(
        per_device, mesh=mesh, in_specs=in_specs, out_specs=out_specs, check_vma=False
    )
```

profile of v0, /device:TPU:0, one launch (start us, length us, event | category | flops | bytes accessed | tf_op | source)
XLA Modules:
  0.0 254.6 jit_solution(12831401750798101958)
XLA Ops:
  7.2 0.0 all-gather.5.cloned.1.call-start
  7.2 0.7 all-gather.5.cloned.1.call-update
  7.9 0.0 reduce-scatter.3.cloned.1.call-start
  7.9 0.7 convert_element_type.40
  8.6 54.6 %all-gather.5.cloned.1.call-done = bf16[2048,1024]{1,0:T(8,128)(2,1)} async-done(((bf16[128,1024]{1,0:T(8,128)(2,1)}), bf16[2048,1024]{1,0:T(8,128)(2,1)}) %all-gather.5.cloned.1.call-update) | async-done | bytes 4194320 | tf_op jit(solution)/shard_map/all_gather | solution.py:13
  63.3 6.2 %fusion.4 = bf16[4,128,2048]{2,1,0:T(8,128)(2,1)} fusion(bf16[2048,1024]{1,0:T(8,128)(2,1)} %all-gather.5.cloned.1.call-done, bf16[4,128,1024]{2,1,0:T(8,128)(2,1)} %param.11, f32[4,1024]{1,0:T(4,128)S(1)} %convert_element_type.40), kind=kOutput, calls=%fused_computation.8 | convolution fusion | flops 2150105088 | bytes 7356416 | tf_op jit(solution)/shard_map/etd,id->eti/dot_general | solution.py:17
  69.5 0.0 copy-start.2
  69.5 0.0 reduce-scatter.3.cloned.1.call-update
  69.5 0.0 all-gather.3.cloned.1.call-start
  69.6 0.6 copy-done.2
  70.2 29.9 %reduce-scatter.3.cloned.1.call-done = bf16[4,128,1024]{2,1,0:T(8,128)(2,1)} async-done(((bf16[4,128,2048]{2,1,0:T(8,128)(2,1)}), bf16[4,128,1024]{2,1,0:T(8,128)(2,1)}) %reduce-scatter.3.cloned.1.call-update) | async-done | bytes 1048592 | tf_op jit(solution)/shard_map/reduce_scatter | solution.py:23
  100.1 0.0 copy-done
  100.1 3.2 %fusion.9 = (f32[4,1024]{1,0:T(4,128)S(1)}, bf16[4,128,1024]{2,1,0:T(8,128)(2,1)}, bf16[4,128,1024]{2,1,0:T(8,128)(2,1)}) fusion(bf16[4,128,1024]{2,1,0:T(8,128)(2,1)} %reduce-scatter.3.cloned.1.call-done, bf16[4,128,1024]{2,1,0:T(8,128)(2,1)S(1)} %copy-done, f32[4,1024]{1,0:T(4,128)S(1)} %convert_element_type.38), kind=kLoop, calls=%fused_computation.14 | loop fusion | flops 4190208 | bytes 4227072 | tf_op jit(solution)/shard_map/reduce_sum | solution.py:27
  103.3 0.0 all-gather.3.cloned.1.call-update
  103.3 0.0 reduce-scatter.5.cloned.1.call-start
  103.4 33.2 %all-gather.3.cloned.1.call-done = bf16[4,128,2048]{2,1,0:T(8,128)(2,1)} async-done(((bf16[4,128,1024]{2,1,0:T(8,128)(2,1)}), bf16[4,128,2048]{2,1,0:T(8,128)(2,1)}) %all-gather.3.cloned.1.call-update) | async-done | bytes 2097168 | tf_op jit(solution)/shard_map/all_gather | solution.py:12
  136.6 0.0 copy-done.4
  136.6 7.2 %convolution_bitcast_fusion = f32[2048,1024]{1,0:T(8,128)} fusion(bf16[4,128,2048]{2,1,0:T(8,128)(2,1)} %all-gather.3.cloned.1.call-done, bf16[4,128,1024]{2,1,0:T(8,128)(2,1)S(1)} %copy-done.4, f32[4,1024]{1,0:T(4,128)S(1)} %convert_element_type.40), kind=kOutput, calls=%fused_computation | convolution fusion | flops 2149056512 | bytes 11550720 | tf_op jit(solution)/shard_map/eti,etd->id/dot_general | solution.py:30
  143.8 0.0 reduce-scatter.5.cloned.1.call-update
  143.8 0.9 copy-done.1
  144.8 0.7 copy-done.3
  145.5 6.6 %convert_reduce_fusion = (f32[128,1024]{1,0:T(8,128)}, f32[4,1024]{1,0:T(4,128)S(1)}, bf16[4,128,1024]{2,1,0:T(8,128)(2,1)}) fusion(bf16[4,128,1024]{2,1,0:T(8,128)(2,1)S(1)} %copy-done.4, f32[4,1024]{1,0:T(4,128)S(1)} %convert_element_type.40, f32[128,1024]{1,0:T(8,128)S(1)} %convert_element_type.36, bf16[4,128,2048]{2,1,0:T(8,128)(2,1)S(1)} %copy-done.3, ...), kind=kOutput, calls=%fused_computation.5 | convolution fusion | flops 2151018496 | bytes 9469952 | tf_op jit(solution)/shard_map/eti,id->etd/dot_general | solution.py:14
  152.1 64.4 %all-reduce = (f32[4,1024]{1,0:T(4,128)}, f32[4,1024]{1,0:T(4,128)}) all-reduce(f32[4,1024]{1,0:T(4,128)S(1)} %get-tuple-element.11, f32[4,1024]{1,0:T(4,128)S(1)} %get-tuple-element.7), channel_id=1, replica_groups=mesh['member'=2,'fsdp'=16] {'fsdp'}, use_global_device_ids=true, to_apply=%region_3.0 | all-reduce | flops 8192 | bytes 65536 | tf_op jit(solution)/shard_map/psum | solution.py:29
  216.5 31.5 %reduce-scatter.5.cloned.1.call-done = f32[128,1024]{1,0:T(8,128)} async-done(((f32[2048,1024]{1,0:T(8,128)}), f32[128,1024]{1,0:T(8,128)}) %reduce-scatter.5.cloned.1.call-update) | async-done | bytes 524304 | tf_op jit(solution)/shard_map/reduce_scatter | solution.py:33
  (6 shorter events, 0.1 us)
Async XLA Ops:
  7.2 56.1 %all-gather.5.cloned.1.call-start = ((), (), s32[]{:S(2)}) async-start(), calls=%async_computation.3 | async-start | bytes 4456448 | tf_op jit(solution)/shard_map/all_gather | solution.py:13
  7.9 92.2 %reduce-scatter.3.cloned.1.call-start = ((), (), s32[]{:S(2)}) async-start(), calls=%async_computation.4 | async-start | bytes 3145728 | tf_op jit(solution)/shard_map/reduce_scatter | solution.py:23
  69.5 0.7 copy-start.2
  69.5 30.6 %copy-start = (bf16[4,128,1024]{2,1,0:T(8,128)(2,1)S(1)}, bf16[4,128,1024]{2,1,0:T(8,128)(2,1)}, u32[]{:S(2)}) copy-start(bf16[4,128,1024]{2,1,0:T(8,128)(2,1)} %param.6) | copy-start | bytes 3145732
  69.5 67.1 %all-gather.3.cloned.1.call-start = ((), (), s32[]{:S(2)}) async-start(), calls=%async_computation.2 | async-start | bytes 3145728 | tf_op jit(solution)/shard_map/all_gather | solution.py:12
  70.2 66.4 %copy-start.4 = (bf16[4,128,1024]{2,1,0:T(8,128)(2,1)S(1)}, bf16[4,128,1024]{2,1,0:T(8,128)(2,1)}, u32[]{:S(2)}) copy-start(bf16[4,128,1024]{2,1,0:T(8,128)(2,1)} %param.11) | copy-start | bytes 3145732
  103.3 144.7 %reduce-scatter.5.cloned.1.call-start = ((), (), s32[]{:S(2)}) async-start(), calls=%async_computation.5 | async-start | bytes 8912896 | tf_op jit(solution)/shard_map/reduce_scatter | solution.py:33
  143.8 0.9 copy-start.1
  143.8 1.7 copy-start.3
Sparse Core Ops, SparseCore 0:
  10.1 53.0 all-gather.4
  69.6 30.4 reduce-scatter.2
  103.5 33.0 all-gather.2
  143.9 104.0 reduce-scatter.4
where the time goes:
time: 255 us
  waiting for transfers between devices  150 us (59%)
  blocking collectives  64.4 us (25%)
  matrix products  20 us (8%)
  between operations  13.8 us (5%)
  other arithmetic  3.96 us (2%)
    psum x1, blocking collectives, per_device(): grad_in, grad_out = lax.psum((grad_in_local, grad_out_local), 'fsdp')  64.4 us
    all_gather x1, waiting for transfers between devices, per_device(): weight = lax.all_gather(out_weight, 'fsdp', axis=0, tiled=True)  54.6 us
    all_gather x1, waiting for transfers between devices, per_device(): scaled_context = lax.all_gather(scaled_local, 'member', axis=2, tiled=True)  33.2 us
    reduce_scatter x1, waiting for transfers between devices, per_device(): lax.psum_scatter(grad_block, 'fsdp', scatter_dimension=0, tiled=True)  31.5 us
    reduce_scatter x1, waiting for transfers between devices, per_device(): lax.psum_scatter(partial_value.astype(jnp.bfloat16), 'member', scatter_di...  29.9 us
    dot_general x1, matrix products, per_device(): jnp.einsum('eti,etd->id', scaled_context, scaled_grad, preferred_element_...  7.2 us
    dot_general x1, matrix products, per_device(): jnp.einsum('eti,id->etd', scaled_context, weight, preferred_element_type=...  6.61 us
    dot_general x1, matrix products, per_device(): jnp.einsum('etd,id->eti', scaled_grad, weight, preferred_element_type=jnp...  6.22 us
  transfers between devices with their start and end apart: 4, of which 4 were waited for; matrix products, arithmetic and copies ran while one was open for 3% of the time, Pallas kernels for 0%

commit v1 on v0

--- a/solution.py
+++ b/solution.py
@@ -9,7 +9,7 @@
     out_wide = out_factor.astype(jnp.float32)
     scaled_local = (context.astype(jnp.float32) * in_wide[:, None, :]).astype(jnp.bfloat16)
     scaled_grad = (cotangent.astype(jnp.float32) * out_wide[:, None, :]).astype(jnp.bfloat16)
-    scaled_context = lax.all_gather(scaled_local, "member", axis=2, tiled=True)
+    scaled_context = jnp.concatenate(lax.all_gather(scaled_local, "member"), axis=2)
     weight = lax.all_gather(out_weight, "fsdp", axis=0, tiled=True)
     projected = jnp.einsum(
         "eti,id->etd", scaled_context, weight, preferred_element_type=jnp.float32

time: 255 us -> 261 us (1.024)
  local copies, waits for them, and re-layouts: 2.24 us -> 8.81 us
    all_gather x0 -> x1, local copies, waits for them, and re-layouts: none -> 3.75 us  [per_device(): lax.all_gather(scaled_local, 'member')]
    reshape x0 -> x1, local copies, waits for them, and re-layouts: none -> 2.82 us  [per_device(): jnp.concatenate(lax.all_gather(scaled_local, 'member'), axis=2)]
where the time goes in v1:
time: 261 us
  waiting for transfers between devices  150 us (57%)
  blocking collectives  64.4 us (25%)
  matrix products  20 us (8%)
  between operations  13.8 us (5%)
  local copies, waits for them, and re-layouts  8.81 us (3%)
  other arithmetic  3.96 us (2%)
    psum x1, blocking collectives, per_device(): grad_in, grad_out = lax.psum((grad_in_local, grad_out_local), 'fsdp')  64.4 us
    all_gather x1, waiting for transfers between devices, per_device(): weight = lax.all_gather(out_weight, 'fsdp', axis=0, tiled=True)  54.6 us
    all_gather x1, waiting for transfers between devices, per_device(): lax.all_gather(scaled_local, 'member')  33.2 us
    reduce_scatter x1, waiting for transfers between devices, per_device(): lax.psum_scatter(grad_block, 'fsdp', scatter_dimension=0, tiled=True)  31.3 us
    reduce_scatter x1, waiting for transfers between devices, per_device(): lax.psum_scatter(partial_value.astype(jnp.bfloat16), 'member', scatter_di...  29.9 us
    dot_general x1, matrix products, per_device(): jnp.einsum('eti,etd->id', scaled_context, scaled_grad, preferred_element_...  7.2 us
    dot_general x1, matrix products, per_device(): jnp.einsum('eti,id->etd', scaled_context, weight, preferred_element_type=...  6.61 us
    dot_general x1, matrix products, per_device(): jnp.einsum('etd,id->eti', scaled_grad, weight, preferred_element_type=jnp...  6.22 us
  transfers between devices with their start and end apart: 4, of which 4 were waited for; matrix products, arithmetic and copies ran while one was open for 3% of the time, Pallas kernels for 0%

profile of v1, /device:TPU:0, one launch (start us, length us, event | category | flops | bytes accessed | tf_op | source)
XLA Modules:
  0.0 260.9 jit_solution(5874129493827920350)
XLA Ops:
  7.2 0.0 all-gather.4.cloned.1.call-start
  7.2 0.7 all-gather.4.cloned.1.call-update
  7.9 0.0 reduce-scatter.3.cloned.1.call-start
  7.9 0.7 convert_element_type.40
  8.6 54.6 %all-gather.4.cloned.1.call-done = bf16[2048,1024]{1,0:T(8,128)(2,1)} async-done(((bf16[128,1024]{1,0:T(8,128)(2,1)}), bf16[2048,1024]{1,0:T(8,128)(2,1)}) %all-gather.4.cloned.1.call-update) | async-done | bytes 4194320 | tf_op jit(solution)/shard_map/all_gather | solution.py:13
  63.3 6.2 %fusion.4 = bf16[4,128,2048]{2,1,0:T(8,128)(2,1)} fusion(bf16[2048,1024]{1,0:T(8,128)(2,1)} %all-gather.4.cloned.1.call-done, bf16[4,128,1024]{2,1,0:T(8,128)(2,1)} %param.11, f32[4,1024]{1,0:T(4,128)S(1)} %convert_element_type.40), kind=kOutput, calls=%fused_computation.8 | convolution fusion | flops 2150105088 | bytes 7356416 | tf_op jit(solution)/shard_map/etd,id->eti/dot_general | solution.py:17
  69.5 0.0 reduce-scatter.3.cloned.1.call-update
  69.5 0.0 all-gather.6.cloned.1.call-start
  69.6 0.6 copy-done.3
  70.2 29.9 %reduce-scatter.3.cloned.1.call-done = bf16[4,128,1024]{2,1,0:T(8,128)(2,1)} async-done(((bf16[4,128,2048]{2,1,0:T(8,128)(2,1)}), bf16[4,128,1024]{2,1,0:T(8,128)(2,1)}) %reduce-scatter.3.cloned.1.call-update) | async-done | bytes 1048592 | tf_op jit(solution)/shard_map/reduce_scatter | solution.py:23
  100.1 3.2 %fusion.9 = (f32[4,1024]{1,0:T(4,128)S(1)}, bf16[4,128,1024]{2,1,0:T(8,128)(2,1)}, bf16[4,128,1024]{2,1,0:T(8,128)(2,1)}) fusion(bf16[4,128,1024]{2,1,0:T(8,128)(2,1)} %reduce-scatter.3.cloned.1.call-done, bf16[4,128,1024]{2,1,0:T(8,128)(2,1)S(1)} %copy-done.1, f32[4,1024]{1,0:T(4,128)S(1)} %convert_element_type.38), kind=kLoop, calls=%fused_computation.14 | loop fusion | flops 4190208 | bytes 4227072 | tf_op jit(solution)/shard_map/reduce_sum | solution.py:27
  103.3 0.0 all-gather.6.cloned.1.call-update
  103.3 0.0 reduce-scatter.5.cloned.1.call-start
  103.4 33.2 %all-gather.6.cloned.1.call-done = bf16[8,128,1024]{2,1,0:T(8,128)(2,1)} async-done(((bf16[4,128,1024]{2,1,0:T(8,128)(2,1)}), bf16[8,128,1024]{2,1,0:T(8,128)(2,1)}) %all-gather.6.cloned.1.call-update) | async-done | bytes 2097168 | tf_op jit(solution)/shard_map/all_gather | solution.py:12
  136.6 3.7 %copy.18 = bf16[2,4,128,1024]{3,0,2,1:T(2,128)(2,1)S(1)} copy(bf16[2,4,128,1024]{3,2,1,0:T(8,128)(2,1)} %bitcast.18) | data formatting | bytes 4194304 | tf_op jit(solution)/shard_map/all_gather | solution.py:12
  140.3 0.0 copy-start.4
  140.4 2.8 %reshape.22 = bf16[4,128,2048]{2,1,0:T(8,128)(2,1)} reshape(bf16[4,128,2,1024]{3,2,1,0:T(2,128)(2,1)S(1)} %bitcast.17) | data formatting | bytes 4194304 | tf_op jit(solution)/shard_map/reshape | solution.py:12
  143.2 7.2 %convolution_bitcast_fusion = f32[2048,1024]{1,0:T(8,128)} fusion(bf16[4,128,2048]{2,1,0:T(8,128)(2,1)} %reshape.22, bf16[4,128,1024]{2,1,0:T(8,128)(2,1)S(1)} %copy-done.4, f32[4,1024]{1,0:T(4,128)S(1)} %convert_element_type.40), kind=kOutput, calls=%fused_computation | convolution fusion | flops 2149056512 | bytes 11550720 | tf_op jit(solution)/shard_map/eti,etd->id/dot_general | solution.py:30
  150.4 0.0 reduce-scatter.5.cloned.1.call-update
  150.4 0.9 copy-done.2
  151.4 0.7 copy-done
  152.1 6.6 %convert_reduce_fusion = (f32[128,1024]{1,0:T(8,128)}, f32[4,1024]{1,0:T(4,128)S(1)}, bf16[4,128,1024]{2,1,0:T(8,128)(2,1)}) fusion(bf16[4,128,1024]{2,1,0:T(8,128)(2,1)S(1)} %copy-done.4, f32[4,1024]{1,0:T(4,128)S(1)} %convert_element_type.40, f32[128,1024]{1,0:T(8,128)S(1)} %convert_element_type.36, bf16[4,128,2048]{2,1,0:T(8,128)(2,1)S(1)} %copy-done, ...), kind=kOutput, calls=%fused_computation.5 | convolution fusion | flops 2151018496 | bytes 9469952 | tf_op jit(solution)/shard_map/eti,id->etd/dot_general | solution.py:14
  158.7 64.4 %all-reduce = (f32[4,1024]{1,0:T(4,128)}, f32[4,1024]{1,0:T(4,128)}) all-reduce(f32[4,1024]{1,0:T(4,128)S(1)} %get-tuple-element.11, f32[4,1024]{1,0:T(4,128)S(1)} %get-tuple-element.7), channel_id=1, replica_groups=mesh['member'=2,'fsdp'=16] {'fsdp'}, use_global_device_ids=true, to_apply=%region_3.0 | all-reduce | flops 8192 | bytes 65536 | tf_op jit(solution)/shard_map/psum | solution.py:29
  223.1 31.3 %reduce-scatter.5.cloned.1.call-done = f32[128,1024]{1,0:T(8,128)} async-done(((f32[2048,1024]{1,0:T(8,128)}), f32[128,1024]{1,0:T(8,128)}) %reduce-scatter.5.cloned.1.call-update) | async-done | bytes 524304 | tf_op jit(solution)/shard_map/reduce_scatter | solution.py:33
  (8 shorter events, 0.1 us)
Async XLA Ops:
  7.2 56.1 %all-gather.4.cloned.1.call-start = ((), (), s32[]{:S(2)}) async-start(), calls=%async_computation.2 | async-start | bytes 4456448 | tf_op jit(solution)/shard_map/all_gather | solution.py:13
  7.9 92.2 %reduce-scatter.3.cloned.1.call-start = ((), (), s32[]{:S(2)}) async-start(), calls=%async_computation.3 | async-start | bytes 3145728 | tf_op jit(solution)/shard_map/reduce_scatter | solution.py:23
  69.5 0.7 copy-start.3
  69.5 30.6 %copy-start.1 = (bf16[4,128,1024]{2,1,0:T(8,128)(2,1)S(1)}, bf16[4,128,1024]{2,1,0:T(8,128)(2,1)}, u32[]{:S(2)}) copy-start(bf16[4,128,1024]{2,1,0:T(8,128)(2,1)} %param.6) | copy-start | bytes 3145732
  69.5 67.1 %all-gather.6.cloned.1.call-start = ((), (), s32[]{:S(2)}) async-start(), calls=%async_computation.5 | async-start | bytes 3145728 | tf_op jit(solution)/shard_map/all_gather | solution.py:12
  103.3 151.0 %reduce-scatter.5.cloned.1.call-start = ((), (), s32[]{:S(2)}) async-start(), calls=%async_computation.4 | async-start | bytes 8912896 | tf_op jit(solution)/shard_map/reduce_scatter | solution.py:33
  140.3 2.8 %copy-start.4 = (bf16[4,128,1024]{2,1,0:T(8,128)(2,1)S(1)}, bf16[4,128,1024]{2,1,0:T(8,128)(2,1)}, u32[]{:S(2)}) copy-start(bf16[4,128,1024]{2,1,0:T(8,128)(2,1)} %param.11) | copy-start | bytes 3145732
  150.4 0.9 copy-start.2
  150.4 1.7 copy-start
Sparse Core Ops, SparseCore 0:
  10.1 53.0 all-gather.3
  69.6 30.4 reduce-scatter.2
  103.5 33.0 all-gather.5
  150.5 103.7 reduce-scatter.4
